TPU v7x, 32 devices: a whole 2x2x4 slice. The times are simulated.
32 devices in a mesh: chain: 8 (over z, y), col: 4 (over x, core).
Axes of the slice: x: 2, y: 2, z: 4, core: 2. Of those that a mesh axis runs over, the one named last changes fastest.
Arguments:
- rhs: bfloat16 [4, 8, 32, 128], P(None, 'chain'), may hold values from -6 to 6
- pattern: int32 [4, 8, 24], P(None, 'chain', 'col'), may hold values from 0 to 31, as said below
- factor: bfloat16 [4, 8, 24, 128, 128], P(None, 'chain', 'col'), may hold values from -0.1875 to 0.1875
- inverse: bfloat16 [4, 8, 128, 128], P(None, 'chain'), as said below
- level_size: int32 [6], replicated, may hold values from 1 to 8, 32 in all
Outputs:
- half_solved: bfloat16 [4, 8, 32, 128], P(None, 'chain')
- solved: bfloat16 [4, 8, 32, 128], P(None, 'chain')
Inputs may be any that keep to these rules, and one draw needn't show every extreme that they name: Among the pattern entries held by one index of chain and one index of col (all 4 of its block rows), at most 3 name block rows on any one index of chain (block row mod 8); in every such group exactly 3 name block rows on one index of chain that is common to all groups of that index of col. A block row may name a block row more than once. `inverse`: each block is lower triangular with a diagonal between 0.3 and 2.
All inputs are finite; a program needn't handle non-finite values.
Results may differ from a plain program's by a relative error of at most 0.013.
Values may be sent and summed in bfloat16 or wider, within the bound.
A program may use at most 64 MiB of HBM per device.

v0:
```python
import jax
import jax.numpy as jnp
from jax import lax
from jax.sharding import PartitionSpec as P


def level_index(positions, ends):
    return jnp.sum((positions[..., None] >= ends).astype(jnp.int32), axis=-1)


def per_device(rhs, pattern, factor, inverse, level_size):
    lane_count = lax.axis_size("chain")
    chain_pos = lax.axis_index("chain")
    row_count = rhs.shape[0]
    probe_count = rhs.shape[2]
    width = rhs.shape[3]
    entries = pattern.shape[2]
    level_count = level_size.shape[0]
    total = row_count * lane_count
    ends = jnp.cumsum(level_size)
    starts = ends - level_size
    own_rows = jnp.arange(row_count, dtype=jnp.int32) * lane_count + chain_pos
    own_level = level_index(own_rows, ends)
    columns = pattern[:, 0, :]
    column_level = level_index(columns, ends)
    keep = column_level < own_level[:, None]
    blocks = factor[:, 0]
    inverse_rows = inverse[:, 0]
    right = rhs[:, 0]
    slot_ids = jnp.arange(row_count, dtype=jnp.int32)
    lane_ids = jnp.arange(lane_count, dtype=jnp.int32)

    def locate(level):
        picked = own_level == level
        own_slot = jnp.sum(jnp.where(picked, slot_ids, 0))
        return (picked, own_slot, jnp.any(picked))

    def forward_level(level, carry):
        store, half_local = carry
        picked, own_slot, is_live = locate(level)
        wanted = keep[own_slot] & is_live
        chosen = jnp.where(
            wanted[:, None, None], store[columns[own_slot]], jnp.zeros((), jnp.bfloat16)
        )
        partial_value = jnp.einsum(
            "jpb,jcb->pc", chosen, blocks[own_slot], preferred_element_type=jnp.float32
        )
        summed = lax.psum(partial_value, "col")
        rest = (right[own_slot].astype(jnp.float32) - summed).astype(jnp.bfloat16)
        segment = jnp.dot(
            rest, inverse_rows[own_slot].T, preferred_element_type=jnp.float32
        ).astype(jnp.bfloat16)
        segment = jnp.where(is_live, segment, jnp.zeros((), jnp.bfloat16))
        front = lax.all_gather(segment[None], "chain", axis=0, tiled=True)
        half_local = jnp.where(picked[:, None, None], segment[None], half_local)
        start = starts[level]
        ordered = front[(start + lane_ids) % lane_count]
        store = lax.dynamic_update_slice_in_dim(store, ordered, start, 0)
        return (store, half_local)

    store = jnp.zeros((total + lane_count, probe_count, width), jnp.bfloat16)
    half_local = jnp.zeros((row_count, probe_count, width), jnp.bfloat16)
    store, half_local = lax.fori_loop(0, level_count, forward_level, (store, half_local))
    solved_local = jnp.zeros((row_count, probe_count, width), jnp.bfloat16)
    count = row_count * entries
    capacity = max(2, (count + lane_count - 1) // lane_count)
    slots_all = lane_count * capacity
    flat_cols = columns.reshape(count)
    flat_src = jnp.broadcast_to(own_rows[:, None], (row_count, entries)).reshape(count)
    dest = flat_cols % lane_count
    onehot = (dest[:, None] == lane_ids[None, :]).astype(jnp.int32)
    before = jnp.cumsum(onehot, axis=0) - onehot
    rank = jnp.sum(before * onehot, axis=1)
    slot = dest * capacity + rank
    select = slot[None, :] == jnp.arange(slots_all, dtype=jnp.int32)[:, None]
    sent_blocks = jnp.dot(
        select.astype(jnp.bfloat16),
        blocks.reshape(count, width * width),
        preferred_element_type=jnp.float32,
    )
    sent_blocks = sent_blocks.astype(jnp.bfloat16).reshape(lane_count, capacity, width, width)
    sent_src = jnp.sum(jnp.where(select, flat_src[None, :] + 1, 0), axis=1) - 1
    sent_dst = jnp.sum(jnp.where(select, flat_cols[None, :] + 1, 0), axis=1) - 1
    sent_meta = jnp.stack([sent_src, sent_dst], axis=1).reshape(lane_count, capacity, 2)
    home_blocks, home_meta = (
        lax.all_to_all(sent_blocks, "chain", split_axis=0, concat_axis=0, tiled=True),
        lax.all_to_all(sent_meta, "chain", split_axis=0, concat_axis=0, tiled=True),
    )
    home_blocks = home_blocks.reshape(slots_all, width, width)
    home_meta = home_meta.reshape(slots_all, 2)
    source_row = home_meta[:, 0]
    target_row = home_meta[:, 1]
    valid = source_row >= 0
    source_level = level_index(source_row, ends)
    target_level = level_index(target_row, ends)
    home_keep = valid & (target_level < source_level)
    source_lane = jnp.where(valid, source_row % lane_count, 0)
    home_slot = jnp.where(valid, target_row // lane_count, -1)

    def home_level(counter, carry):
        accum, solved_now = carry
        level = level_count - 1 - counter
        picked, own_slot, is_live = locate(level)
        summed = lax.psum(accum[own_slot], "col")
        rest = (half_local[own_slot].astype(jnp.float32) - summed).astype(jnp.bfloat16)
        segment = jnp.dot(rest, inverse_rows[own_slot], preferred_element_type=jnp.float32).astype(
            jnp.bfloat16
        )
        segment = jnp.where(is_live, segment, jnp.zeros((), jnp.bfloat16))
        solved_now = jnp.where(picked[:, None, None], segment[None], solved_now)
        front = lax.all_gather(segment[None], "chain", axis=0, tiled=True)
        active = home_keep & (source_level == level)
        incoming = front[source_lane]
        terms = jnp.einsum(
            "kpc,kcb->kpb", incoming, home_blocks, preferred_element_type=jnp.float32
        )
        spread = ((home_slot[None, :] == slot_ids[:, None]) & active[None, :]).astype(jnp.float32)
        added = jnp.dot(
            spread,
            terms.reshape(slots_all, probe_count * width),
            precision=lax.Precision.HIGHEST,
            preferred_element_type=jnp.float32,
        )
        accum = accum + added.reshape(row_count, probe_count, width)
        return (accum, solved_now)

    accum = jnp.zeros((row_count, probe_count, width), jnp.float32)
    accum, solved_local = lax.fori_loop(0, level_count, home_level, (accum, solved_local))
    return (half_local[:, None], solved_local[:, None])


def solution(mesh):
    return jax.shard_map(
        per_device,
        mesh=mesh,
        in_specs=(
            P(None, "chain", None, None),
            P(None, "chain", "col"),
            P(None, "chain", "col", None, None),
            P(None, "chain", None, None),
            P(),
        ),
        out_specs=(P(None, "chain", None, None), P(None, "chain", None, None)),
        check_vma=False,
    )
```

profile of v0, /device:TPU:0, one launch (start us, length us, event | category | flops | bytes accessed | tf_op | source)
XLA Modules:
  0.0 617.3 jit_solution(10101479652952594900)
XLA Ops:
  23.2 314.8 %while.35 = (s32[]{:T(128)}, bf16[40,32,128]{2,1,0:T(8,128)(2,1)S(1)}, bf16[4,32,128]{2,1,0:T(8,128)(2,1)S(1)}, s32[4]{0:T(128)S(1)}, bf16[4,32,128]{2,1,0:T(8,1...) while((s32[]{:T(128)}, ...), condition=%wide.region_7.8_spmd.clone, body=%wide.region_3.7_spmd.clone.sunk | while | flops 7424167 | bytes 878571 | solution.py:63
  29.5 10.4 %psum.30 = f32[32,128]{1,0:T(8,128)S(1)} all-reduce(f32[32,128]{1,0:T(8,128)S(1)} %convolution_bitcast_fusion.2), channel_id=1, replica_groups=mesh['chain'=8,'col'=4] {'col'}, use_global_device_ids=true, to_apply=%region_6.6 | all-reduce | flops 4096 | bytes 32768 | tf_op jit(solution)/shard_map/while/body/eval_jaxpr/psum | solution.py:48
  41.4 31.1 %all-gather.6 = bf16[256,128]{1,0:T(8,128)(2,1)S(1)} all-gather(bf16[32,128]{1,0:T(8,128)(2,1)S(1)} %fusion.84), channel_id=2, replica_groups=mesh['chain'=8,'col'=4] {'chain'}, dimensions={0}, use_global_device_ids=true | all-gather | bytes 73728 | tf_op jit(solution)/shard_map/while/body/eval_jaxpr/all_gather | solution.py:54
  82.6 10.1 %psum.30 = f32[32,128]{1,0:T(8,128)S(1)} all-reduce(f32[32,128]{1,0:T(8,128)S(1)} %convolution_bitcast_fusion.2), channel_id=1, replica_groups=mesh['chain'=8,'col'=4] {'col'}, use_global_device_ids=true, to_apply=%region_6.6 | all-reduce | flops 4096 | bytes 32768 | tf_op jit(solution)/shard_map/while/body/eval_jaxpr/psum | solution.py:48
  94.2 30.6 %all-gather.6 = bf16[256,128]{1,0:T(8,128)(2,1)S(1)} all-gather(bf16[32,128]{1,0:T(8,128)(2,1)S(1)} %fusion.84), channel_id=2, replica_groups=mesh['chain'=8,'col'=4] {'chain'}, dimensions={0}, use_global_device_ids=true | all-gather | bytes 73728 | tf_op jit(solution)/shard_map/while/body/eval_jaxpr/all_gather | solution.py:54
  135.0 10.1 %psum.30 = f32[32,128]{1,0:T(8,128)S(1)} all-reduce(f32[32,128]{1,0:T(8,128)S(1)} %convolution_bitcast_fusion.2), channel_id=1, replica_groups=mesh['chain'=8,'col'=4] {'col'}, use_global_device_ids=true, to_apply=%region_6.6 | all-reduce | flops 4096 | bytes 32768 | tf_op jit(solution)/shard_map/while/body/eval_jaxpr/psum | solution.py:48
  146.6 30.6 %all-gather.6 = bf16[256,128]{1,0:T(8,128)(2,1)S(1)} all-gather(bf16[32,128]{1,0:T(8,128)(2,1)S(1)} %fusion.84), channel_id=2, replica_groups=mesh['chain'=8,'col'=4] {'chain'}, dimensions={0}, use_global_device_ids=true | all-gather | bytes 73728 | tf_op jit(solution)/shard_map/while/body/eval_jaxpr/all_gather | solution.py:54
  187.3 10.1 %psum.30 = f32[32,128]{1,0:T(8,128)S(1)} all-reduce(f32[32,128]{1,0:T(8,128)S(1)} %convolution_bitcast_fusion.2), channel_id=1, replica_groups=mesh['chain'=8,'col'=4] {'col'}, use_global_device_ids=true, to_apply=%region_6.6 | all-reduce | flops 4096 | bytes 32768 | tf_op jit(solution)/shard_map/while/body/eval_jaxpr/psum | solution.py:48
  198.9 30.6 %all-gather.6 = bf16[256,128]{1,0:T(8,128)(2,1)S(1)} all-gather(bf16[32,128]{1,0:T(8,128)(2,1)S(1)} %fusion.84), channel_id=2, replica_groups=mesh['chain'=8,'col'=4] {'chain'}, dimensions={0}, use_global_device_ids=true | all-gather | bytes 73728 | tf_op jit(solution)/shard_map/while/body/eval_jaxpr/all_gather | solution.py:54
  239.6 10.1 %psum.30 = f32[32,128]{1,0:T(8,128)S(1)} all-reduce(f32[32,128]{1,0:T(8,128)S(1)} %convolution_bitcast_fusion.2), channel_id=1, replica_groups=mesh['chain'=8,'col'=4] {'col'}, use_global_device_ids=true, to_apply=%region_6.6 | all-reduce | flops 4096 | bytes 32768 | tf_op jit(solution)/shard_map/while/body/eval_jaxpr/psum | solution.py:48
  251.2 30.6 %all-gather.6 = bf16[256,128]{1,0:T(8,128)(2,1)S(1)} all-gather(bf16[32,128]{1,0:T(8,128)(2,1)S(1)} %fusion.84), channel_id=2, replica_groups=mesh['chain'=8,'col'=4] {'chain'}, dimensions={0}, use_global_device_ids=true | all-gather | bytes 73728 | tf_op jit(solution)/shard_map/while/body/eval_jaxpr/all_gather | solution.py:54
  291.9 10.1 %psum.30 = f32[32,128]{1,0:T(8,128)S(1)} all-reduce(f32[32,128]{1,0:T(8,128)S(1)} %convolution_bitcast_fusion.2), channel_id=1, replica_groups=mesh['chain'=8,'col'=4] {'col'}, use_global_device_ids=true, to_apply=%region_6.6 | all-reduce | flops 4096 | bytes 32768 | tf_op jit(solution)/shard_map/while/body/eval_jaxpr/psum | solution.py:48
  303.6 30.6 %all-gather.6 = bf16[256,128]{1,0:T(8,128)(2,1)S(1)} all-gather(bf16[32,128]{1,0:T(8,128)(2,1)S(1)} %fusion.84), channel_id=2, replica_groups=mesh['chain'=8,'col'=4] {'chain'}, dimensions={0}, use_global_device_ids=true | all-gather | bytes 73728 | tf_op jit(solution)/shard_map/while/body/eval_jaxpr/all_gather | solution.py:54
  338.2 278.4 %while.36 = (s32[]{:T(128)}, f32[4,32,128]{2,0,1:T(4,128)S(1)}, bf16[4,32,128]{2,1,0:T(8,128)(2,1)S(1)}, s32[24]{0:T(128)S(1)}, s32[24]{0:T(128)S(1)}, /*index=5...) while((s32[]{:T(128)}, f32[4,32,128]{2,0,1:T(4,128)S(1)}, ...), condition=%wide.region_18.19_spmd.clone.clone, body=%wide.region_14.18_spmd.clone.clone.sunk | while | flops 31024460 | bytes 2709372 | solution.py:128
  341.7 10.1 %psum.31 = f32[32,128]{1,0:T(8,128)S(1)} all-reduce(f32[32,128]{1,0:T(8,128)S(1)} %bitcast.150), channel_id=1, replica_groups=mesh['chain'=8,'col'=4] {'col'}, use_global_device_ids=true, to_apply=%region_17.17 | all-reduce | flops 4096 | bytes 32768 | tf_op jit(solution)/shard_map/while/body/eval_jaxpr/psum | solution.py:104
  352.6 30.5 %all-gather.7 = bf16[256,128]{1,0:T(8,128)(2,1)S(1)} all-gather(bf16[32,128]{1,0:T(8,128)(2,1)S(1)} %fusion.94), channel_id=3, replica_groups=mesh['chain'=8,'col'=4] {'chain'}, dimensions={0}, use_global_device_ids=true | all-gather | bytes 73728 | tf_op jit(solution)/shard_map/while/body/eval_jaxpr/all_gather | solution.py:111
  388.1 10.1 %psum.31 = f32[32,128]{1,0:T(8,128)S(1)} all-reduce(f32[32,128]{1,0:T(8,128)S(1)} %bitcast.150), channel_id=1, replica_groups=mesh['chain'=8,'col'=4] {'col'}, use_global_device_ids=true, to_apply=%region_17.17 | all-reduce | flops 4096 | bytes 32768 | tf_op jit(solution)/shard_map/while/body/eval_jaxpr/psum | solution.py:104
  399.0 30.5 %all-gather.7 = bf16[256,128]{1,0:T(8,128)(2,1)S(1)} all-gather(bf16[32,128]{1,0:T(8,128)(2,1)S(1)} %fusion.94), channel_id=3, replica_groups=mesh['chain'=8,'col'=4] {'chain'}, dimensions={0}, use_global_device_ids=true | all-gather | bytes 73728 | tf_op jit(solution)/shard_map/while/body/eval_jaxpr/all_gather | solution.py:111
  434.5 10.1 %psum.31 = f32[32,128]{1,0:T(8,128)S(1)} all-reduce(f32[32,128]{1,0:T(8,128)S(1)} %bitcast.150), channel_id=1, replica_groups=mesh['chain'=8,'col'=4] {'col'}, use_global_device_ids=true, to_apply=%region_17.17 | all-reduce | flops 4096 | bytes 32768 | tf_op jit(solution)/shard_map/while/body/eval_jaxpr/psum | solution.py:104
  445.4 30.5 %all-gather.7 = bf16[256,128]{1,0:T(8,128)(2,1)S(1)} all-gather(bf16[32,128]{1,0:T(8,128)(2,1)S(1)} %fusion.94), channel_id=3, replica_groups=mesh['chain'=8,'col'=4] {'chain'}, dimensions={0}, use_global_device_ids=true | all-gather | bytes 73728 | tf_op jit(solution)/shard_map/while/body/eval_jaxpr/all_gather | solution.py:111
  480.9 10.1 %psum.31 = f32[32,128]{1,0:T(8,128)S(1)} all-reduce(f32[32,128]{1,0:T(8,128)S(1)} %bitcast.150), channel_id=1, replica_groups=mesh['chain'=8,'col'=4] {'col'}, use_global_device_ids=true, to_apply=%region_17.17 | all-reduce | flops 4096 | bytes 32768 | tf_op jit(solution)/shard_map/while/body/eval_jaxpr/psum | solution.py:104
  491.8 30.5 %all-gather.7 = bf16[256,128]{1,0:T(8,128)(2,1)S(1)} all-gather(bf16[32,128]{1,0:T(8,128)(2,1)S(1)} %fusion.94), channel_id=3, replica_groups=mesh['chain'=8,'col'=4] {'chain'}, dimensions={0}, use_global_device_ids=true | all-gather | bytes 73728 | tf_op jit(solution)/shard_map/while/body/eval_jaxpr/all_gather | solution.py:111
  538.2 30.5 %all-gather.7 = bf16[256,128]{1,0:T(8,128)(2,1)S(1)} all-gather(bf16[32,128]{1,0:T(8,128)(2,1)S(1)} %fusion.94), channel_id=3, replica_groups=mesh['chain'=8,'col'=4] {'chain'}, dimensions={0}, use_global_device_ids=true | all-gather | bytes 73728 | tf_op jit(solution)/shard_map/while/body/eval_jaxpr/all_gather | solution.py:111
  584.6 30.5 %all-gather.7 = bf16[256,128]{1,0:T(8,128)(2,1)S(1)} all-gather(bf16[32,128]{1,0:T(8,128)(2,1)S(1)} %fusion.94), channel_id=3, replica_groups=mesh['chain'=8,'col'=4] {'chain'}, dimensions={0}, use_global_device_ids=true | all-gather | bytes 73728 | tf_op jit(solution)/shard_map/while/body/eval_jaxpr/all_gather | solution.py:111
  (205 shorter events, 111.8 us)
Async XLA Ops:
  4.0 13.8 %all-to-all-start = ((s32[8,3,2]{1,2,0:T(2,128)}), s32[8,3,2]{1,2,0:T(2,128)S(1)}, u32[]{:S(2)}, u32[]{:S(2)}) async-start(s32[8,3,2]{1,2,0:T(2,128)} %copy.16), calls=%async_computation | async-start | bytes 16384 | tf_op jit(solution)/shard_map/all_to_all | solution.py:87
  17.8 5.3 copy-start.2
  17.8 320.4 %all-to-all-start.1 = ((bf16[8,3,128,128]{3,2,1,0:T(8,128)(2,1)}), bf16[8,3,128,128]{3,2,1,0:T(8,128)(2,1)S(1)}, u32[]{:S(2)}, u32[]{:S(2)}) async-start(bf16[8,3,128,128]{3,2,1,0:T(8,128)(2,1)} %bitcast.42), calls=%async_computation.1 | async-start | bytes 1572864 | tf_op jit(solution)/shard_map/all_to_all | solution.py:86
  616.6 0.6 copy-start
  616.6 0.6 copy-start.1
where the time goes:
time: 619 us; the launch traced here: 617 us
  blocking collectives  489 us (79%)
  loops' own time  36 us (6%)
  other arithmetic  33.2 us (5%)
  matrix products  26.7 us (4%)
  local copies, waits for them, and re-layouts  18.2 us (3%)
  starting transfers between devices  12.6 us (2%)
    all_gather x6, blocking collectives, forward_level(): front = lax.all_gather(segment[None], 'chain', axis=0, tiled=True)  184 us
    all_gather x6, blocking collectives, home_level(): front = lax.all_gather(segment[None], 'chain', axis=0, tiled=True)  183 us
    psum x6, blocking collectives, forward_level(): summed = lax.psum(partial_value, 'col')  61.1 us
    psum x6, blocking collectives, home_level(): summed = lax.psum(accum[own_slot], 'col')  60.7 us
    another operation x1, loops' own time, per_device(): lax.fori_loop(0, level_count, forward_level, (store, half_local))  23.3 us
    another operation x1, loops' own time, per_device(): lax.fori_loop(0, level_count, home_level, (accum, solved_local))  12.7 us
  transfers between devices with their start and end apart: 2, of which 1 were waited for; matrix products, arithmetic and copies ran while one was open for 8% of the time, Pallas kernels for 0%

commit v1 on v0

--- a/solution.py
+++ b/solution.py
@@ -108,7 +108,23 @@
         )
         segment = jnp.where(is_live, segment, jnp.zeros((), jnp.bfloat16))
         solved_now = jnp.where(picked[:, None, None], segment[None], solved_now)
-        front = lax.all_gather(segment[None], "chain", axis=0, tiled=True)
+
+        def clear_the_panels(m, axis_id):
+            e_now = lax.axis_index(axis_id)
+            right_arr = lax.axis_size(axis_id)
+            passed, z1 = (right_arr, e_now)
+            prior, everything = (m, 1)
+            while everything < passed:
+                work_now = lax.ppermute(
+                    prior, axis_name=axis_id, perm=[(it, it ^ everything) for it in range(passed)]
+                )
+                local_out = jnp.concatenate([prior, work_now], axis=0)
+                high = jnp.concatenate([work_now, prior], axis=0)
+                prior = jnp.where(z1 & everything == 0, local_out, high)
+                everything = 2 * everything
+            return prior
+
+        front = clear_the_panels(segment[None], "chain")
         active = home_keep & (source_level == level)
         incoming = front[source_lane]
         terms = jnp.einsum(

time: 619 us -> 510 us (0.82)
  blocking collectives: 489 us -> 306 us
  waiting for transfers between devices: 0.85 us -> 57.5 us
  starting transfers between devices: 12.6 us -> 29.2 us
    all_gather x6 -> x0, blocking collectives: 183 us -> none  [home_level(): front = lax.all_gather(segment[None], 'chain', axis=0, tiled=True)]
    ppermute x0 -> x18, waiting for transfers between devices: none -> 56.7 us  [clear_the_panels(): lax.ppermute(prior, axis_name=axis_id, perm=[(it, it ^ everything) for it...]
    ppermute x0 -> x18, starting transfers between devices: none -> 16.6 us  [clear_the_panels(): lax.ppermute(prior, axis_name=axis_id, perm=[(it, it ^ everything) for it...]
  transfers between devices with their start and end apart: 2 -> 20, of which waited for: 1 -> 19; matrix products, arithmetic and copies ran while one was open for 8% -> 10% of each run, Pallas kernels for 0% -> 0%
where the time goes in v1:
time: 510 us; the launch traced here: 508 us
  blocking collectives  306 us (60%)
  waiting for transfers between devices  57.5 us (11%)
  loops' own time  36.2 us (7%)
  other arithmetic  33.3 us (7%)
  starting transfers between devices  29.2 us (6%)
  matrix products  26.7 us (5%)
  local copies, waits for them, and re-layouts  18.2 us (4%)
    all_gather x6, blocking collectives, forward_level(): front = lax.all_gather(segment[None], 'chain', axis=0, tiled=True)  184 us
    psum x6, blocking collectives, forward_level(): summed = lax.psum(partial_value, 'col')  61.1 us
    psum x6, blocking collectives, home_level(): summed = lax.psum(accum[own_slot], 'col')  60.7 us
    ppermute x18, waiting for transfers between devices, clear_the_panels(): lax.ppermute(prior, axis_name=axis_id, perm=[(it, it ^ everything) for it...  56.7 us
    another operation x1, loops' own time, per_device(): lax.fori_loop(0, level_count, forward_level, (store, half_local))  23.3 us
    ppermute x18, starting transfers between devices, clear_the_panels(): lax.ppermute(prior, axis_name=axis_id, perm=[(it, it ^ everything) for it...  16.6 us
    another operation x1, loops' own time, per_device(): lax.fori_loop(0, level_count, home_level, (accum, solved_local))  12.9 us
  transfers between devices with their start and end apart: 20, of which 19 were waited for; matrix products, arithmetic and copies ran while one was open for 10% of the time, Pallas kernels for 0%

profile of v1, /device:TPU:0, one launch (start us, length us, event | category | flops | bytes accessed | tf_op | source)
XLA Modules:
  0.0 507.6 jit_solution(1890398373732575165)
XLA Ops:
  4.0 7.3 %all-to-all-start = ((s32[8,3,2]{1,2,0:T(2,128)}), s32[8,3,2]{1,2,0:T(2,128)S(1)}, u32[]{:S(2)}, u32[]{:S(2)}) async-start(s32[8,3,2]{1,2,0:T(2,128)} %copy.16), calls=%async_computation | async-start | bytes 16384 | tf_op jit(solution)/shard_map/all_to_all | solution.py:87
  17.8 5.3 %all-to-all-start.1 = ((bf16[8,3,128,128]{3,2,1,0:T(8,128)(2,1)}), bf16[8,3,128,128]{3,2,1,0:T(8,128)(2,1)S(1)}, u32[]{:S(2)}, u32[]{:S(2)}) async-start(bf16[8,3,128,128]{3,2,1,0:T(8,128)(2,1)} %bitcast.42), calls=%async_computation.1 | async-start | bytes 1572864 | tf_op jit(solution)/shard_map/all_to_all | solution.py:86
  23.2 314.8 %while.35 = (s32[]{:T(128)}, bf16[40,32,128]{2,1,0:T(8,128)(2,1)S(1)}, bf16[4,32,128]{2,1,0:T(8,128)(2,1)S(1)}, s32[4]{0:T(128)S(1)}, bf16[4,32,128]{2,1,0:T(8,1...) while((s32[]{:T(128)}, ...), condition=%wide.region_7.8_spmd.clone, body=%wide.region_3.7_spmd.clone.sunk | while | flops 7424167 | bytes 878571 | solution.py:63
  29.5 10.4 %psum.30 = f32[32,128]{1,0:T(8,128)S(1)} all-reduce(f32[32,128]{1,0:T(8,128)S(1)} %convolution_bitcast_fusion.2), channel_id=1, replica_groups=mesh['chain'=8,'col'=4] {'col'}, use_global_device_ids=true, to_apply=%region_6.6 | all-reduce | flops 4096 | bytes 32768 | tf_op jit(solution)/shard_map/while/body/eval_jaxpr/psum | solution.py:48
  41.4 31.1 %all-gather.3 = bf16[256,128]{1,0:T(8,128)(2,1)S(1)} all-gather(bf16[32,128]{1,0:T(8,128)(2,1)S(1)} %fusion.84), channel_id=2, replica_groups=mesh['chain'=8,'col'=4] {'chain'}, dimensions={0}, use_global_device_ids=true | all-gather | bytes 73728 | tf_op jit(solution)/shard_map/while/body/eval_jaxpr/all_gather | solution.py:54
  82.6 10.1 %psum.30 = f32[32,128]{1,0:T(8,128)S(1)} all-reduce(f32[32,128]{1,0:T(8,128)S(1)} %convolution_bitcast_fusion.2), channel_id=1, replica_groups=mesh['chain'=8,'col'=4] {'col'}, use_global_device_ids=true, to_apply=%region_6.6 | all-reduce | flops 4096 | bytes 32768 | tf_op jit(solution)/shard_map/while/body/eval_jaxpr/psum | solution.py:48
  94.2 30.6 %all-gather.3 = bf16[256,128]{1,0:T(8,128)(2,1)S(1)} all-gather(bf16[32,128]{1,0:T(8,128)(2,1)S(1)} %fusion.84), channel_id=2, replica_groups=mesh['chain'=8,'col'=4] {'chain'}, dimensions={0}, use_global_device_ids=true | all-gather | bytes 73728 | tf_op jit(solution)/shard_map/while/body/eval_jaxpr/all_gather | solution.py:54
  135.0 10.1 %psum.30 = f32[32,128]{1,0:T(8,128)S(1)} all-reduce(f32[32,128]{1,0:T(8,128)S(1)} %convolution_bitcast_fusion.2), channel_id=1, replica_groups=mesh['chain'=8,'col'=4] {'col'}, use_global_device_ids=true, to_apply=%region_6.6 | all-reduce | flops 4096 | bytes 32768 | tf_op jit(solution)/shard_map/while/body/eval_jaxpr/psum | solution.py:48
  146.6 30.6 %all-gather.3 = bf16[256,128]{1,0:T(8,128)(2,1)S(1)} all-gather(bf16[32,128]{1,0:T(8,128)(2,1)S(1)} %fusion.84), channel_id=2, replica_groups=mesh['chain'=8,'col'=4] {'chain'}, dimensions={0}, use_global_device_ids=true | all-gather | bytes 73728 | tf_op jit(solution)/shard_map/while/body/eval_jaxpr/all_gather | solution.py:54
  187.3 10.1 %psum.30 = f32[32,128]{1,0:T(8,128)S(1)} all-reduce(f32[32,128]{1,0:T(8,128)S(1)} %convolution_bitcast_fusion.2), channel_id=1, replica_groups=mesh['chain'=8,'col'=4] {'col'}, use_global_device_ids=true, to_apply=%region_6.6 | all-reduce | flops 4096 | bytes 32768 | tf_op jit(solution)/shard_map/while/body/eval_jaxpr/psum | solution.py:48
  198.9 30.6 %all-gather.3 = bf16[256,128]{1,0:T(8,128)(2,1)S(1)} all-gather(bf16[32,128]{1,0:T(8,128)(2,1)S(1)} %fusion.84), channel_id=2, replica_groups=mesh['chain'=8,'col'=4] {'chain'}, dimensions={0}, use_global_device_ids=true | all-gather | bytes 73728 | tf_op jit(solution)/shard_map/while/body/eval_jaxpr/all_gather | solution.py:54
  239.6 10.1 %psum.30 = f32[32,128]{1,0:T(8,128)S(1)} all-reduce(f32[32,128]{1,0:T(8,128)S(1)} %convolution_bitcast_fusion.2), channel_id=1, replica_groups=mesh['chain'=8,'col'=4] {'col'}, use_global_device_ids=true, to_apply=%region_6.6 | all-reduce | flops 4096 | bytes 32768 | tf_op jit(solution)/shard_map/while/body/eval_jaxpr/psum | solution.py:48
  251.2 30.6 %all-gather.3 = bf16[256,128]{1,0:T(8,128)(2,1)S(1)} all-gather(bf16[32,128]{1,0:T(8,128)(2,1)S(1)} %fusion.84), channel_id=2, replica_groups=mesh['chain'=8,'col'=4] {'chain'}, dimensions={0}, use_global_device_ids=true | all-gather | bytes 73728 | tf_op jit(solution)/shard_map/while/body/eval_jaxpr/all_gather | solution.py:54
  291.9 10.1 %psum.30 = f32[32,128]{1,0:T(8,128)S(1)} all-reduce(f32[32,128]{1,0:T(8,128)S(1)} %convolution_bitcast_fusion.2), channel_id=1, replica_groups=mesh['chain'=8,'col'=4] {'col'}, use_global_device_ids=true, to_apply=%region_6.6 | all-reduce | flops 4096 | bytes 32768 | tf_op jit(solution)/shard_map/while/body/eval_jaxpr/psum | solution.py:48
  303.6 30.6 %all-gather.3 = bf16[256,128]{1,0:T(8,128)(2,1)S(1)} all-gather(bf16[32,128]{1,0:T(8,128)(2,1)S(1)} %fusion.84), channel_id=2, replica_groups=mesh['chain'=8,'col'=4] {'chain'}, dimensions={0}, use_global_device_ids=true | all-gather | bytes 73728 | tf_op jit(solution)/shard_map/while/body/eval_jaxpr/all_gather | solution.py:54
  338.2 168.8 %while.36 = (s32[]{:T(128)}, f32[4,32,128]{2,0,1:T(4,128)S(1)}, bf16[4,32,128]{2,1,0:T(8,128)(2,1)S(1)}, s32[24]{0:T(128)S(1)}, s32[24]{0:T(128)S(1)}, /*index=5...) while((s32[]{:T(128)}, f32[4,32,128]{2,0,1:T(4,128)S(1)}, ...), condition=%wide.region_18.19_spmd.clone.clone, body=%wide.region_14.18_spmd.clone.clone.sunk | while | flops 31196500 | bytes 3094638 | solution.py:144
  341.7 10.1 %psum.31 = f32[32,128]{1,0:T(8,128)S(1)} all-reduce(f32[32,128]{1,0:T(8,128)S(1)} %bitcast.151), channel_id=1, replica_groups=mesh['chain'=8,'col'=4] {'col'}, use_global_device_ids=true, to_apply=%region_17.17 | all-reduce | flops 4096 | bytes 32768 | tf_op jit(solution)/shard_map/while/body/eval_jaxpr/psum | solution.py:104
  369.9 10.1 %psum.31 = f32[32,128]{1,0:T(8,128)S(1)} all-reduce(f32[32,128]{1,0:T(8,128)S(1)} %bitcast.151), channel_id=1, replica_groups=mesh['chain'=8,'col'=4] {'col'}, use_global_device_ids=true, to_apply=%region_17.17 | all-reduce | flops 4096 | bytes 32768 | tf_op jit(solution)/shard_map/while/body/eval_jaxpr/psum | solution.py:104
  398.0 10.1 %psum.31 = f32[32,128]{1,0:T(8,128)S(1)} all-reduce(f32[32,128]{1,0:T(8,128)S(1)} %bitcast.151), channel_id=1, replica_groups=mesh['chain'=8,'col'=4] {'col'}, use_global_device_ids=true, to_apply=%region_17.17 | all-reduce | flops 4096 | bytes 32768 | tf_op jit(solution)/shard_map/while/body/eval_jaxpr/psum | solution.py:104
  426.1 10.1 %psum.31 = f32[32,128]{1,0:T(8,128)S(1)} all-reduce(f32[32,128]{1,0:T(8,128)S(1)} %bitcast.151), channel_id=1, replica_groups=mesh['chain'=8,'col'=4] {'col'}, use_global_device_ids=true, to_apply=%region_17.17 | all-reduce | flops 4096 | bytes 32768 | tf_op jit(solution)/shard_map/while/body/eval_jaxpr/psum | solution.py:104
  454.2 10.1 %psum.31 = f32[32,128]{1,0:T(8,128)S(1)} all-reduce(f32[32,128]{1,0:T(8,128)S(1)} %bitcast.151), channel_id=1, replica_groups=mesh['chain'=8,'col'=4] {'col'}, use_global_device_ids=true, to_apply=%region_17.17 | all-reduce | flops 4096 | bytes 32768 | tf_op jit(solution)/shard_map/while/body/eval_jaxpr/psum | solution.py:104
  473.6 3.7 collective-permute-done.2
  482.3 10.1 %psum.31 = f32[32,128]{1,0:T(8,128)S(1)} all-reduce(f32[32,128]{1,0:T(8,128)S(1)} %bitcast.151), channel_id=1, replica_groups=mesh['chain'=8,'col'=4] {'col'}, use_global_device_ids=true, to_apply=%region_17.17 | all-reduce | flops 4096 | bytes 32768 | tf_op jit(solution)/shard_map/while/body/eval_jaxpr/psum | solution.py:104
  501.8 3.8 collective-permute-done.2
  (253 shorter events, 144.8 us)
Async XLA Ops:
  4.0 13.8 %all-to-all-start = ((s32[8,3,2]{1,2,0:T(2,128)}), s32[8,3,2]{1,2,0:T(2,128)S(1)}, u32[]{:S(2)}, u32[]{:S(2)}) async-start(s32[8,3,2]{1,2,0:T(2,128)} %copy.16), calls=%async_computation | async-start | bytes 16384 | tf_op jit(solution)/shard_map/all_to_all | solution.py:87
  17.8 5.3 %copy-start.2 = (bf16[4,1,128,128]{3,2,1,0:T(8,128)(2,1)S(1)}, bf16[4,1,128,128]{3,2,1,0:T(8,128)(2,1)}, u32[]{:S(2)}) copy-start(bf16[4,1,128,128]{3,2,1,0:T(8,128)(2,1)} %param.12) | copy-start | bytes 393220
  17.8 320.4 %all-to-all-start.1 = ((bf16[8,3,128,128]{3,2,1,0:T(8,128)(2,1)}), bf16[8,3,128,128]{3,2,1,0:T(8,128)(2,1)S(1)}, u32[]{:S(2)}, u32[]{:S(2)}) async-start(bf16[8,3,128,128]{3,2,1,0:T(8,128)(2,1)} %bitcast.42), calls=%async_computation.1 | async-start | bytes 1572864 | tf_op jit(solution)/shard_map/all_to_all | solution.py:86
  352.6 3.7 collective-permute-start
  356.3 3.7 collective-permute-start.1
  360.0 5.0 collective-permute-start.2
  380.8 3.7 collective-permute-start
  384.5 3.7 collective-permute-start.1
  388.2 4.9 collective-permute-start.2
  408.9 3.7 collective-permute-start
  412.6 3.7 collective-permute-start.1
  416.3 4.9 collective-permute-start.2
  437.0 3.7 collective-permute-start
  440.7 3.7 collective-permute-start.1
  444.4 4.9 collective-permute-start.2
  465.1 3.7 collective-permute-start
  468.7 3.7 collective-permute-start.1
  472.5 4.9 collective-permute-start.2
  493.2 3.7 collective-permute-start
  496.8 3.7 collective-permute-start.1
  500.6 5.0 collective-permute-start.2
  507.0 0.6 copy-start
  507.0 0.6 copy-start.1
